TPU v7x, 512 devices: a whole 4x8x8 slice. The times are simulated.
512 devices in a mesh: grow: 32 (over x_hi, y, core), gcol: 16 (over z, x_lo).
Axes of the slice: x: 4 (x_hi: 2, x_lo: 2; x = x_hi * 2 + x_lo), y: 8, z: 8, core: 2. Of those that a mesh axis runs over, the one named last changes fastest.
Arguments:
- coefficients: bfloat16 [20480, 49152], P('grow', 'gcol'), may hold values from -0.02734375 to 0.02734375
- tile_mask: int32 [160, 384], P('grow', 'gcol'), may hold values 0 or 1
- duals: float32 [20480], P('grow'), may hold values from -6 to 6
- costs: float32 [49152], P('gcol'), may hold values from -6 to 6
- primal: float32 [49152], P('gcol'), may hold values from 0.1 to 10
- fixed: int32 [49152], P('gcol'), may hold values 0 or 1
Outputs:
- normal_window: float32 [1024, 20480], P('gcol', 'grow')
- factor_window: float32 [1024, 20480], P('gcol', 'grow')
All inputs are finite; a program needn't handle non-finite values. No bound on the sum of `tile_mask` or of `fixed` on one device may be relied on, other than what follows from the above.
Results may differ from a plain program's by a relative error of at most 0.0023.
Values may be sent and summed in bfloat16 or wider, within the bound.
A program may use at most 64 MiB of HBM per device.

v0:
```python
import jax
import jax.numpy as jnp
from jax import lax
from jax.sharding import PartitionSpec as P

PANEL = 512
SOFTNESS = 0.25
DIAGONAL_SHIFT = 0.5


def split_normal(normal, blocks_own, panel_per, rows_dev):
    split = normal.reshape(blocks_own, 2, panel_per, rows_dev)
    own_panel = split[:, 0].reshape(blocks_own * panel_per, rows_dev)
    own_trailing = split[:, 1].reshape(blocks_own * panel_per, rows_dev)
    panel_all = lax.all_gather(own_panel, "gcol", axis=0, tiled=True)
    return (own_trailing, panel_all)


def shards(coefficients, tile_mask, duals, costs, primal, fixed):
    rows_dev, columns = coefficients.shape
    row_count = lax.axis_size("grow")
    col_count = lax.axis_size("gcol")
    panel_per = PANEL // row_count
    blocks_own = row_count // col_count
    local_win = blocks_own * 2 * panel_per
    tile_rows, tile_cols = tile_mask.shape
    side = rows_dev // tile_rows
    expanded = jnp.broadcast_to(
        tile_mask[:, None, :, None], (tile_rows, side, tile_cols, side)
    ).reshape(rows_dev, columns)
    masked = coefficients * expanded.astype(jnp.bfloat16)
    partial_products = jnp.dot(
        duals, masked, preferred_element_type=jnp.float32, precision=lax.Precision.HIGHEST
    )
    products = lax.psum(partial_products, "grow")
    reduced = costs - products
    scaling = (1 - fixed).astype(jnp.float32) * primal / jnp.sqrt(reduced * reduced + SOFTNESS)
    scaled = (masked * scaling[None, :]).astype(jnp.bfloat16)
    window_all = lax.all_gather(masked[: 2 * panel_per], "grow", axis=0, tiled=True)
    col_index = lax.axis_index("gcol")
    normal = lax.psum_scatter(
        lax.dot_general(
            window_all, scaled, (((1,), (1,)), ((), ())), preferred_element_type=jnp.float32
        ),
        "gcol",
        scatter_dimension=0,
        tiled=True,
    )
    own_trailing, panel_all = split_normal(normal, blocks_own, panel_per, rows_dev)
    corner = lax.all_gather(panel_all[:, :panel_per], "grow", axis=1, tiled=True)
    shifted = 0.5 * (corner + corner.T) + DIAGONAL_SHIFT * jnp.eye(PANEL, dtype=jnp.float32)
    lower = jnp.linalg.cholesky(shifted)
    factor_panel = jax.scipy.linalg.solve_triangular(lower, panel_all, lower=True)
    edge_all = lax.all_gather(
        factor_panel[:, panel_per : 2 * panel_per], "grow", axis=1, tiled=True
    )
    own_edge = lax.dynamic_slice_in_dim(
        edge_all, col_index * (blocks_own * panel_per), blocks_own * panel_per, 1
    )
    updated = own_trailing - jnp.dot(own_edge.T, factor_panel, precision=lax.Precision.HIGHEST)
    panel_rows = lax.dynamic_slice_in_dim(
        factor_panel, col_index * (blocks_own * panel_per), blocks_own * panel_per, 0
    )
    factor = jnp.stack(
        [
            panel_rows.reshape(blocks_own, panel_per, rows_dev),
            updated.reshape(blocks_own, panel_per, rows_dev),
        ],
        axis=1,
    )
    return (normal, factor.reshape(local_win, rows_dev))


def solution(mesh):
    placed = (P("grow", "gcol"), P("grow", "gcol"), P("grow"), P("gcol"), P("gcol"), P("gcol"))
    return jax.shard_map(
        shards,
        mesh=mesh,
        in_specs=placed,
        out_specs=(P("gcol", "grow"), P("gcol", "grow")),
        check_vma=False,
    )
```

profile of v0, /device:TPU:1, one launch (start us, length us, event | category | flops | bytes accessed | tf_op | source)
XLA Modules:
  0.0 642.4 jit_solution(5346488050266648543)
XLA Ops:
  7.2 0.8 convert_element_type.17
  8.6 0.7 copy-done.2
  9.9 1.9 copy-done
  11.8 0.7 slice.145
  12.6 3.7 fusion.38
  16.3 130.1 %psum.7 = f32[3072]{0:T(1024)S(1)} all-reduce(f32[3072]{0:T(1024)S(1)} %bitcast.77), channel_id=1, replica_groups=mesh['grow'=32,'gcol'=16] {'grow'}, use_global_device_ids=true, to_apply=%region_0.0 | all-reduce | flops 3072 | bytes 24576 | tf_op jit(solution)/shard_map/psum | solution.py:35
  146.5 9.5 %fusion = f32[1024,640]{1,0:T(8,128)} fusion(bf16[1024,3072]{1,0:T(8,128)(2,1)} %all-gather.5.cloned.1.call-done, bf16[640,3072]{1,0:T(8,128)(2,1)} %copy-done, f32[3072]{0:T(1024)S(1)} %rsqrt_multiply_fusion), kind=kOutput, calls=%fused_computation.3 | convolution fusion | flops 4032430080 | bytes 12857344 | tf_op jit(solution)/shard_map/dot_general | solution.py:42
  156.0 74.2 %reduce-scatter.2.cloned.1.call-done = f32[64,640]{1,0:T(8,128)} async-done(((f32[1024,640]{1,0:T(8,128)}), f32[64,640]{1,0:T(8,128)}) %reduce-scatter.2.cloned.1.call-update) | async-done | bytes 163856 | tf_op jit(solution)/shard_map/reduce_scatter | solution.py:41
  230.3 1.6 fusion.37
  231.9 71.6 %all-gather.7.cloned.1.call-done = f32[512,640]{1,0:T(8,128)} async-done(((f32[32,640]{1,0:T(8,128)}), f32[512,640]{1,0:T(8,128)}) %all-gather.7.cloned.1.call-update) | async-done | bytes 1310736 | tf_op jit(solution)/shard_map/all_gather | solution.py:15
  303.5 1.0 slice.147
  304.5 0.7 copy.24
  305.8 94.8 %all-gather.9.cloned.1.call-done = f32[512,512]{0,1:T(8,128)} async-done(((f32[512,16]{0,1:T(8,128)}), f32[512,512]{0,1:T(8,128)}) %all-gather.9.cloned.1.call-update) | async-done | bytes 1048592 | tf_op jit(solution)/shard_map/all_gather | solution.py:50
  400.6 1.6 copy.19
  403.1 11.7 %cholesky.103 = f32[128,128]{1,0:T(8,128)S(1)} custom-call(f32[128,128]{1,0:T(8,128)S(1)} %cholesky.263), custom_call_target="Cholesky" | custom-call | tf_op jit(solution)/shard_map/jit(cholesky)/cholesky | solution.py:52
  414.8 9.8 %custom-call.31 = f32[1,128,128]{1,2,0:T(8,128)S(1)} custom-call(f32[1,128,128]{2,1,0:T(8,128)S(1)} %get-tuple-element.31), custom_call_target="InvertDiagBlocksLowerTriangular" | custom-call | tf_op jit(solution)/shard_map/jit(cholesky)/cholesky | solution.py:52
  425.1 1.0 convolution_subtract_fusion.3
  426.1 0.9 cholesky.267
  427.1 11.7 %cholesky.215 = f32[128,128]{1,0:T(8,128)S(1)} custom-call(f32[128,128]{1,0:T(8,128)S(1)} %cholesky.267), custom_call_target="Cholesky" | custom-call | tf_op jit(solution)/shard_map/jit(cholesky)/cholesky | solution.py:52
  438.8 9.9 %custom-call.32 = f32[1,128,128]{1,2,0:T(8,128)S(1)} custom-call(f32[1,128,128]{2,1,0:T(8,128)S(1)} %get-tuple-element.28), custom_call_target="InvertDiagBlocksLowerTriangular" | custom-call | tf_op jit(solution)/shard_map/jit(cholesky)/cholesky | solution.py:52
  448.7 1.2 convolution_dynamic-update-slice_fusion
  450.3 0.6 cholesky.272
  450.9 13.2 %cholesky.236 = f32[128,128]{1,0:T(8,128)} custom-call(f32[128,128]{1,0:T(8,128)} %cholesky.272), custom_call_target="Cholesky" | custom-call | tf_op jit(solution)/shard_map/jit(cholesky)/cholesky | solution.py:52
  464.1 1.5 select_reduce_fusion.1
  465.6 0.7 compare_reduce_fusion.1
  466.3 11.3 %custom-call.33 = f32[1,128,128]{1,2,0:T(8,128)} custom-call(f32[1,128,128]{2,1,0:T(8,128)} %get-tuple-element.25), custom_call_target="InvertDiagBlocksLowerTriangular" | custom-call | tf_op jit(solution)/shard_map/jit(cholesky)/cholesky | solution.py:52
  477.6 1.0 convolution_dynamic-update-slice_fusion.1
  479.0 11.9 %cholesky.253 = f32[128,128]{1,0:T(8,128)S(1)} custom-call(f32[128,128]{1,0:T(8,128)S(1)} %convolution_subtract_fusion.6), custom_call_target="Cholesky" | custom-call | tf_op jit(solution)/shard_map/jit(cholesky)/cholesky | solution.py:52
  490.9 0.7 compare_reduce_fusion
  491.7 0.6 compare_reduce_fusion.2
  494.9 10.7 %while.1 = (s32[]{:T(128)}, f32[512,512]{1,0:T(8,128)S(1)}, s32[4,2]{0,1:T(2,128)S(1)}, f32[4,128,128]{2,1,0:T(8,128)}, s32[]{:T(128)}) while((s32[]{:T(128)}, f32[512,512]{1,0:T(8,128)S(1)}, s32[4,2]{0,1:T(2,128)S(1)}, f32[4,128,128]{2,1,0:T(8,128)}, s32[]{:T(128)}) %tuple.32), condition=%wide.while_cond, body=%wide.while_body.sunk | while | flops 2 | bytes 132705 | solution.py:53
  495.0 0.6 fusion.48
  495.6 2.0 bitcast_dynamic-update-slice_fusion.2
  497.6 0.6 fusion.48
  498.2 2.0 bitcast_dynamic-update-slice_fusion.2
  500.3 0.6 fusion.48
  500.9 2.0 bitcast_dynamic-update-slice_fusion.2
  503.0 0.6 fusion.48
  503.6 2.0 bitcast_dynamic-update-slice_fusion.2
  505.6 40.1 %custom-call.34 = f32[4,128,128]{1,2,0:T(8,128)S(1)} custom-call(f32[4,128,128]{2,1,0:T(8,128)} %get-tuple-element.9), custom_call_target="InvertDiagBlocksLowerTriangular" | custom-call | tf_op jit(solution)/shard_map/jit(_solve_triangular)/triangular_solve | solution.py:53
  546.8 1.3 fusion.26
  548.7 1.3 fusion.24
  550.0 0.9 convolution_subtract_fusion.2
  550.9 1.3 fusion.23
  552.4 0.7 copy.21
  553.2 80.1 %all-gather.11.cloned.1.call-done = f32[512,512]{0,1:T(8,128)} async-done(((f32[512,16]{0,1:T(8,128)}), f32[512,512]{0,1:T(8,128)}) %all-gather.11.cloned.1.call-update) | async-done | bytes 1048592 | tf_op jit(solution)/shard_map/all_gather | solution.py:54
  633.3 1.7 convolution_subtract_fusion.5
  635.0 0.7 copy.22
  (59 shorter events, 6.3 us)
Async XLA Ops:
  7.2 139.3 %all-gather.5.cloned.1.call-start = ((), (), s32[]{:S(2)}) async-start(), calls=%async_computation.1 | async-start | bytes 6488064 | tf_op jit(solution)/shard_map/all_gather | solution.py:39
  7.2 2.1 copy-start.2
  9.3 3.2 copy-start.9
  9.9 1.9 copy-start
  11.8 134.6 %copy-start.6 = (f32[3072]{0:T(1024)S(1)}, f32[3072]{0:T(1024)}, u32[]{:S(2)}) copy-start(f32[3072]{0:T(1024)} %param.9) | copy-start | bytes 36868
  11.8 134.6 %copy-start.7 = (f32[3072]{0:T(1024)S(1)}, f32[3072]{0:T(1024)}, u32[]{:S(2)}) copy-start(f32[3072]{0:T(1024)} %param.10) | copy-start | bytes 36868
  11.8 134.6 %copy-start.8 = (s32[3072]{0:T(1024)S(1)}, s32[3072]{0:T(1024)}, u32[]{:S(2)}) copy-start(s32[3072]{0:T(1024)} %param.11) | copy-start | bytes 36868
  12.5 217.7 %reduce-scatter.2.cloned.1.call-start = ((), (), s32[]{:S(2)}) async-start(), calls=%async_computation.2 | async-start | bytes 2785280 | tf_op jit(solution)/shard_map/reduce_scatter | solution.py:41
  156.0 147.6 %all-gather.7.cloned.1.call-start = ((), (), s32[]{:S(2)}) async-start(), calls=%async_computation.3 | async-start | bytes 1392640 | tf_op jit(solution)/shard_map/all_gather | solution.py:15
  231.9 168.7 %all-gather.9.cloned.1.call-start = ((), (), s32[]{:S(2)}) async-start(), calls=%async_computation.4 | async-start | bytes 1081344 | tf_op jit(solution)/shard_map/all_gather | solution.py:50
  305.3 328.0 %all-gather.11.cloned.1.call-start = ((), (), s32[]{:S(2)}) async-start(), calls=%async_computation.5 | async-start | bytes 1081344 | tf_op jit(solution)/shard_map/all_gather | solution.py:54
  400.6 1.7 copy-start.1
  426.1 119.6 %copy-start.3 = (f32[512,640]{1,0:T(8,128)S(1)}, f32[512,640]{1,0:T(8,128)}, u32[]{:S(2)}) copy-start(f32[512,640]{1,0:T(8,128)} %all-gather.7.cloned.1.call-done) | copy-start | bytes 3932164
  545.7 0.7 copy-start.4
  550.8 82.4 %copy-start.5 = (f32[2,1,16,640]{3,2,1,0:T(8,128)S(1)}, f32[2,1,16,640]{3,2,1,0:T(8,128)}, u32[]{:S(2)}) copy-start(f32[2,1,16,640]{3,2,1,0:T(8,128)} %get-tuple-element.21) | copy-start | bytes 245764
Sparse Core Ops, SparseCore 0:
  12.6 105.7 all-gather.4
  156.1 74.1 reduce-scatter.1
  232.9 70.5 all-gather.6
  307.3 93.2 all-gather.8
  553.3 79.9 all-gather.10
where the time goes:
time: 648 us; the launch traced here: 642 us
  waiting for transfers between devices  321 us (50%)
  blocking collectives  130 us (20%)
  other arithmetic  125 us (19%)
  matrix products  25.4 us (4%)
  local copies, waits for them, and re-layouts  23.3 us (4%)
  between operations  16.8 us (3%)
    psum x1, blocking collectives, shards(): products = lax.psum(partial_products, 'grow')  130 us
    all_gather x1, waiting for transfers between devices, shards(): lax.all_gather(panel_all[:, :panel_per], 'grow', axis=1, tiled=True)  94.8 us
    another operation x14, other arithmetic, shards(): lower = jnp.linalg.cholesky(shifted)  83.1 us
    all_gather x1, waiting for transfers between devices, shards(): lax.all_gather(factor_panel[:, panel_per:2 * panel_per], 'grow', axis=1,...  80.1 us
    reduce_scatter x1, waiting for transfers between devices, shards(): lax.psum_scatter(lax.dot_general(window_all, scaled, (((1,), (1,)), ((),...  74.2 us
    all_gather x1, waiting for transfers between devices, split_normal(): panel_all = lax.all_gather(own_panel, 'gcol', axis=0, tiled=True)  71.6 us
    another operation x4, other arithmetic, shards(): jax.scipy.linalg.solve_triangular(lower, panel_all, lower=True)  40.3 us
  transfers between devices with their start and end apart: 5, of which 4 were waited for; matrix products, arithmetic and copies ran while one was open for 1% of the time, Pallas kernels for 0%

commit v1 on v0

--- a/solution.py
+++ b/solution.py
@@ -12,7 +12,9 @@
     split = normal.reshape(blocks_own, 2, panel_per, rows_dev)
     own_panel = split[:, 0].reshape(blocks_own * panel_per, rows_dev)
     own_trailing = split[:, 1].reshape(blocks_own * panel_per, rows_dev)
-    panel_all = lax.all_gather(own_panel, "gcol", axis=0, tiled=True)
+    panel_all = jnp.concatenate(
+        lax.all_to_all(jnp.stack([own_panel] * lax.axis_size("gcol")), "gcol", 0, 0), axis=0
+    )
     return (own_trailing, panel_all)
 
 

time: 648 us -> 588 us (0.907)
  waiting for transfers between devices: 321 us -> 243 us
  blocking collectives: 130 us -> 158 us
    all_gather x1 -> x0, waiting for transfers between devices: 71.6 us -> none  [split_normal(): panel_all = lax.all_gather(own_panel, 'gcol', axis=0, tiled=True)]
    all_to_all x0 -> x1, blocking collectives: none -> 27.9 us  [split_normal(): lax.all_to_all(jnp.stack([own_panel] * lax.axis_size('gcol')), 'gcol', 0, 0)]
    all_gather x1, waiting for transfers between devices: 94.8 us -> 88.3 us  [shards(): lax.all_gather(panel_all[:, :panel_per], 'grow', axis=1, tiled=True)]
  transfers between devices with their start and end apart: 5 -> 4, of which waited for: 4 -> 3; matrix products, arithmetic and copies ran while one was open for 1% -> 1% of each run, Pallas kernels for 0% -> 0%
where the time goes in v1:
time: 588 us; the launch traced here: 583 us
  waiting for transfers between devices  243 us (41%)
  blocking collectives  158 us (27%)
  other arithmetic  121 us (21%)
  matrix products  22.1 us (4%)
  local copies, waits for them, and re-layouts  20.8 us (4%)
  between operations  16.9 us (3%)
    psum x1, blocking collectives, shards(): products = lax.psum(partial_products, 'grow')  130 us
    all_gather x1, waiting for transfers between devices, shards(): lax.all_gather(panel_all[:, :panel_per], 'grow', axis=1, tiled=True)  88.3 us
    all_gather x1, waiting for transfers between devices, shards(): lax.all_gather(factor_panel[:, panel_per:2 * panel_per], 'grow', axis=1,...  80.1 us
    another operation x14, other arithmetic, shards(): lower = jnp.linalg.cholesky(shifted)  78.7 us
    reduce_scatter x1, waiting for transfers between devices, shards(): lax.psum_scatter(lax.dot_general(window_all, scaled, (((1,), (1,)), ((),...  74.2 us
    another operation x4, other arithmetic, shards(): jax.scipy.linalg.solve_triangular(lower, panel_all, lower=True)  40.9 us
    all_to_all x1, blocking collectives, split_normal(): lax.all_to_all(jnp.stack([own_panel] * lax.axis_size('gcol')), 'gcol', 0, 0)  27.9 us
  transfers between devices with their start and end apart: 4, of which 3 were waited for; matrix products, arithmetic and copies ran while one was open for 1% of the time, Pallas kernels for 0%

profile of v1, /device:TPU:1, one launch (start us, length us, event | category | flops | bytes accessed | tf_op | source)
XLA Modules:
  0.0 582.6 jit_solution(14502172686337505011)
XLA Ops:
  7.2 0.8 convert_element_type.17
  8.1 0.6 broadcast_in_dim.3
  8.6 0.7 copy-done.2
  9.3 0.5 bitcast_multiply_fusion
  9.9 1.9 copy-done
  11.8 0.7 slice.149
  12.6 3.7 fusion.38
  16.3 130.1 %psum.7 = f32[3072]{0:T(1024)S(1)} all-reduce(f32[3072]{0:T(1024)S(1)} %bitcast.86), channel_id=1, replica_groups=mesh['grow'=32,'gcol'=16] {'grow'}, use_global_device_ids=true, to_apply=%region_0.0 | all-reduce | flops 3072 | bytes 24576 | tf_op jit(solution)/shard_map/psum | solution.py:37
  146.5 9.5 %fusion = f32[1024,640]{1,0:T(8,128)} fusion(bf16[1024,3072]{1,0:T(8,128)(2,1)} %all-gather.4.cloned.1.call-done, bf16[640,3072]{1,0:T(8,128)(2,1)} %copy-done, f32[3072]{0:T(1024)S(1)} %rsqrt_multiply_fusion), kind=kOutput, calls=%fused_computation.3 | convolution fusion | flops 4032430080 | bytes 12857344 | tf_op jit(solution)/shard_map/dot_general | solution.py:44
  156.0 74.2 %reduce-scatter.2.cloned.1.call-done = f32[64,640]{1,0:T(8,128)} async-done(((f32[1024,640]{1,0:T(8,128)}), f32[64,640]{1,0:T(8,128)}) %reduce-scatter.2.cloned.1.call-update) | async-done | bytes 163856 | tf_op jit(solution)/shard_map/reduce_scatter | solution.py:43
  230.3 0.9 fusion.37
  231.3 27.9 %all_to_all.5 = f32[16,32,640]{2,1,0:T(8,128)S(1)} all-to-all(f32[16,32,640]{2,1,0:T(8,128)S(1)} %stack.6), channel_id=1, replica_groups=mesh['grow'=32,'gcol'=16] {'gcol'}, dimensions={0} | all-to-all | bytes 2621440 | tf_op jit(solution)/shard_map/all_to_all | solution.py:16
  259.2 0.7 copy.21
  260.0 0.5 all-gather.8.cloned.1.call-start
  260.5 0.6 iota_multiply_fusion
  261.1 1.0 fusion.36
  262.1 88.3 %all-gather.6.cloned.1.call-done = f32[512,512]{0,1:T(8,128)} async-done(((f32[512,16]{0,1:T(8,128)}), f32[512,512]{0,1:T(8,128)}) %all-gather.6.cloned.1.call-update) | async-done | bytes 1048592 | tf_op jit(solution)/shard_map/all_gather | solution.py:52
  350.4 1.6 copy.17
  352.9 11.7 %cholesky.103 = f32[128,128]{1,0:T(8,128)S(1)} custom-call(f32[128,128]{1,0:T(8,128)S(1)} %cholesky.263), custom_call_target="Cholesky" | custom-call | tf_op jit(solution)/shard_map/jit(cholesky)/cholesky | solution.py:54
  364.7 9.8 %custom-call.31 = f32[1,128,128]{1,2,0:T(8,128)S(1)} custom-call(f32[1,128,128]{2,1,0:T(8,128)S(1)} %get-tuple-element.35), custom_call_target="InvertDiagBlocksLowerTriangular" | custom-call | tf_op jit(solution)/shard_map/jit(cholesky)/cholesky | solution.py:54
  375.3 11.7 %cholesky.215 = f32[128,128]{1,0:T(8,128)S(1)} custom-call(f32[128,128]{1,0:T(8,128)S(1)} %cholesky.267), custom_call_target="Cholesky" | custom-call | tf_op jit(solution)/shard_map/jit(cholesky)/cholesky | solution.py:54
  387.0 10.0 %custom-call.32 = f32[1,128,128]{1,2,0:T(8,128)S(1)} custom-call(f32[1,128,128]{2,1,0:T(8,128)S(1)} %get-tuple-element.32), custom_call_target="InvertDiagBlocksLowerTriangular" | custom-call | tf_op jit(solution)/shard_map/jit(cholesky)/cholesky | solution.py:54
  397.7 11.7 %cholesky.236 = f32[128,128]{1,0:T(8,128)S(1)} custom-call(f32[128,128]{1,0:T(8,128)S(1)} %cholesky.272), custom_call_target="Cholesky" | custom-call | tf_op jit(solution)/shard_map/jit(cholesky)/cholesky | solution.py:54
  409.4 0.7 compare_reduce_fusion.1
  410.1 9.8 %custom-call.33 = f32[1,128,128]{1,2,0:T(8,128)S(1)} custom-call(f32[1,128,128]{2,1,0:T(8,128)S(1)} %get-tuple-element.29), custom_call_target="InvertDiagBlocksLowerTriangular" | custom-call | tf_op jit(solution)/shard_map/jit(cholesky)/cholesky | solution.py:54
  420.5 11.9 %cholesky.253 = f32[128,128]{1,0:T(8,128)S(1)} custom-call(f32[128,128]{1,0:T(8,128)S(1)} %convolution_subtract_fusion.6), custom_call_target="Cholesky" | custom-call | tf_op jit(solution)/shard_map/jit(cholesky)/cholesky | solution.py:54
  432.4 0.6 compare_reduce_fusion
  433.1 0.7 compare_reduce_fusion.2
  436.5 10.4 %while.1 = (s32[]{:T(128)}, f32[512,512]{1,0:T(8,128)S(1)}, s32[4,2]{0,1:T(2,128)S(1)}, f32[4,128,128]{2,1,0:T(8,128)}, s32[]{:T(128)}) while((s32[]{:T(128)}, f32[512,512]{1,0:T(8,128)S(1)}, s32[4,2]{0,1:T(2,128)S(1)}, f32[4,128,128]{2,1,0:T(8,128)}, s32[]{:T(128)}) %tuple.35), condition=%wide.while_cond, body=%wide.while_body.sunk | while | flops 2 | bytes 132705 | solution.py:55
  436.5 0.5 fusion.49
  437.1 2.0 bitcast_dynamic-update-slice_fusion.2
  439.1 0.5 fusion.49
  439.7 2.0 bitcast_dynamic-update-slice_fusion.2
  441.7 0.5 fusion.49
  442.2 2.0 bitcast_dynamic-update-slice_fusion.2
  444.3 0.5 fusion.49
  444.8 2.0 bitcast_dynamic-update-slice_fusion.2
  446.8 40.1 %custom-call.34 = f32[4,128,128]{1,2,0:T(8,128)S(1)} custom-call(f32[4,128,128]{2,1,0:T(8,128)} %get-tuple-element.9), custom_call_target="InvertDiagBlocksLowerTriangular" | custom-call | tf_op jit(solution)/shard_map/jit(_solve_triangular)/triangular_solve | solution.py:55
  487.0 0.5 fusion.25
  487.9 0.5 fusion.24
  488.4 0.5 convolution_subtract_fusion
  488.9 1.3 fusion.22
  490.2 0.9 convolution_subtract_fusion.2
  491.1 1.3 fusion.21
  492.6 0.7 copy.19
  493.4 80.1 %all-gather.8.cloned.1.call-done = f32[512,512]{0,1:T(8,128)} async-done(((f32[512,16]{0,1:T(8,128)}), f32[512,512]{0,1:T(8,128)}) %all-gather.8.cloned.1.call-update) | async-done | bytes 1048592 | tf_op jit(solution)/shard_map/all_gather | solution.py:56
  573.5 1.7 convolution_subtract_fusion.5
  575.2 0.7 copy.20
  (63 shorter events, 4.4 us)
Async XLA Ops:
  7.2 139.3 %all-gather.4.cloned.1.call-start = ((), (), s32[]{:S(2)}) async-start(), calls=%async_computation.2 | async-start | bytes 6488064 | tf_op jit(solution)/shard_map/all_gather | solution.py:41
  7.2 2.1 copy-start.2
  9.3 3.2 copy-start.10
  9.9 1.9 copy-start
  11.8 134.6 %copy-start.7 = (f32[3072]{0:T(1024)S(1)}, f32[3072]{0:T(1024)}, u32[]{:S(2)}) copy-start(f32[3072]{0:T(1024)} %param.9) | copy-start | bytes 36868
  11.8 134.6 %copy-start.8 = (f32[3072]{0:T(1024)S(1)}, f32[3072]{0:T(1024)}, u32[]{:S(2)}) copy-start(f32[3072]{0:T(1024)} %param.10) | copy-start | bytes 36868
  11.8 134.6 %copy-start.9 = (s32[3072]{0:T(1024)S(1)}, s32[3072]{0:T(1024)}, u32[]{:S(2)}) copy-start(s32[3072]{0:T(1024)} %param.11) | copy-start | bytes 36868
  12.5 217.7 %reduce-scatter.2.cloned.1.call-start = ((), (), s32[]{:S(2)}) async-start(), calls=%async_computation.3 | async-start | bytes 2785280 | tf_op jit(solution)/shard_map/reduce_scatter | solution.py:43
  156.0 194.5 %all-gather.6.cloned.1.call-start = ((), (), s32[]{:S(2)}) async-start(), calls=%async_computation.4 | async-start | bytes 1081344 | tf_op jit(solution)/shard_map/all_gather | solution.py:52
  260.0 313.5 %all-gather.8.cloned.1.call-start = ((), (), s32[]{:S(2)}) async-start(), calls=%async_computation.5 | async-start | bytes 1081344 | tf_op jit(solution)/shard_map/all_gather | solution.py:56
  350.4 1.7 copy-start.1
  374.9 61.5 %copy-start.11 = (s32[4]{0:T(128)S(1)}, s32[4]{0:T(128)}, u32[]{:S(2)}) copy-start(s32[4]{0:T(128)} %iota_multiply_fusion) | copy-start | bytes 52
  375.3 111.7 %copy-start.4 = (f32[4,32,640]{2,1,0:T(8,128)S(1)}, f32[4,32,640]{2,1,0:T(8,128)}, u32[]{:S(2)}) copy-start(f32[4,32,640]{2,1,0:T(8,128)} %get-tuple-element.20) | copy-start | bytes 983044
  397.3 90.2 %copy-start.3 = (f32[4,32,640]{2,1,0:T(8,128)S(1)}, f32[4,32,640]{2,1,0:T(8,128)}, u32[]{:S(2)}) copy-start(f32[4,32,640]{2,1,0:T(8,128)} %get-tuple-element.23) | copy-start | bytes 983044
  436.3 52.1 %copy-start.5 = (f32[4,32,640]{2,1,0:T(8,128)S(1)}, f32[4,32,640]{2,1,0:T(8,128)}, u32[]{:S(2)}) copy-start(f32[4,32,640]{2,1,0:T(8,128)} %get-tuple-element.22) | copy-start | bytes 983044
  486.9 1.4 copy-start.6
Sparse Core Ops, SparseCore 0:
  12.6 105.7 all-gather.3
  156.1 74.1 reduce-scatter.1
  260.1 90.2 all-gather.5
  493.5 79.9 all-gather.7
